TPU v7x, 512 devices: a whole 4x4x16 slice. The times are simulated.
512 devices in a mesh: ctx: 8 (over y, z_hi), tp: 64 (over x, z_lo, core).
Axes of the slice: x: 4, y: 4, z: 16 (z_hi: 2, z_lo: 8; z = z_hi * 8 + z_lo), core: 2. Of those that a mesh axis runs over, the one named last changes fastest.
Arguments:
- hidden: bfloat16 [2048, 2048], P(('ctx', 'tp')), may hold values from -6 to 6
- w_in: bfloat16 [2048, 8192], P(None, 'tp'), may hold values from -0.125 to 0.125
- w_bc: bfloat16 [2048, 32], replicated, may hold values from -0.125 to 0.125
- w_dt: bfloat16 [64, 2048], P('tp'), may hold values from -0.125 to 0.125
- dt_bias: float32 [64], P('tp'), may hold values from -5 to -3
- a_log: float32 [64], P('tp'), may hold values from -4.6 to 0
- d_skip: float32 [64], P('tp'), may hold values from 0.5 to 1.5
- conv_w: float32 [4, 4096], P(None, 'tp'), may hold values from -3 to 3
- w_out: bfloat16 [4096, 2048], P('tp'), may hold values from -0.09375 to 0.09375
- d_out: bfloat16 [2048, 2048], P(('ctx', 'tp')), may hold values from -6 to 6
Outputs:
- d_hidden: bfloat16 [2048, 2048], P(('ctx', 'tp'))
- d_w_in: float32 [2048, 8192], P(None, 'tp')
- d_w_out: float32 [4096, 2048], P('tp')
- d_w_bc: float32 [2048, 32], replicated
All inputs are finite; a program needn't handle non-finite values.
Results may differ from a plain program's by a relative error of at most 0.017.
Values may be sent and summed in bfloat16 or wider, within the bound.
A program may use at most 64 MiB of HBM per device.

v0:
```python
import math
import jax
import jax.numpy as jnp
from jax import lax
from jax.sharding import PartitionSpec as P

STATE = 16
CONV = 4
precise = lax.Precision.HIGHEST


def padded(array, sides, width):
    for axis, dim in sides:
        size, length = (lax.axis_size(axis), array.shape[dim])
        up = [(i, (i + 1) % size) for i in range(size - 1)]
        down = [(j, i) for i, j in up]
        last = lax.slice_in_dim(array, length - width, length, axis=dim)
        leading = lax.slice_in_dim(array, 0, width, axis=dim)
        before = lax.ppermute(last, axis, up)
        after = lax.ppermute(leading, axis, down)
        array = jnp.concatenate([before, array, after], axis=dim)
    return array


def entering(array, axis, combine, identity, reverse):
    length, index = (lax.axis_size(axis), lax.axis_index(axis))
    everything = jax.tree.map(lambda part: lax.all_gather(part, axis), array)
    start = jax.tree.map(
        lambda part, zero: jnp.broadcast_to(jnp.asarray(zero, part.dtype), part.shape),
        array,
        identity,
    )

    def step(k, before):
        at = length - 1 - k if reverse else k
        reached = at > index if reverse else at < index
        new = combine(before, jax.tree.map(lambda part: part[at], everything))
        return jax.tree.map(lambda a, b: jnp.where(reached, a, b), new, before)

    return lax.fori_loop(0, length, step, start)


def times_rows(operand_a, operand_b):
    return lax.dot_general(
        operand_a, operand_b, (((1,), (1,)), ((), ())), preferred_element_type=jnp.float32
    )


def across_rows(operand_a, operand_b):
    return lax.dot_general(
        operand_a, operand_b, (((0,), (0,)), ((), ())), preferred_element_type=jnp.float32
    )


def conv_silu(x_ext, conv_w):
    length = x_ext.shape[0] - CONV + 1
    summed = conv_w[0] * x_ext[0:length]
    for shift_k in range(1, CONV):
        summed = summed + conv_w[shift_k] * x_ext[shift_k : shift_k + length]
    return jax.nn.silu(summed)


def block_ssd(conv_out, steps_dt, b_rows, c_rows, decay_rate, state_in):
    positions = conv_out.shape[0]
    log_keep = jnp.cumsum(steps_dt * decay_rate)
    causal = lax.broadcasted_iota(jnp.int32, (positions, positions), 0) >= lax.broadcasted_iota(
        jnp.int32, (positions, positions), 1
    )
    decays = jnp.exp(jnp.where(causal, log_keep[:, None] - log_keep[None, :], -jnp.inf))
    scores = jnp.einsum("in,jn->ij", c_rows, b_rows, precision=precise) * decays
    weighted = steps_dt[:, None] * conv_out
    outputs = jnp.einsum("ij,jp->ip", scores, weighted, precision=precise)
    outputs = outputs + jnp.exp(log_keep)[:, None] * jnp.einsum(
        "in,pn->ip", c_rows, state_in, precision=precise
    )
    remains = jnp.exp(log_keep[-1] - log_keep)
    state_out = jnp.exp(log_keep[-1]) * state_in + jnp.einsum(
        "j,jp,jn->pn", remains, weighted, b_rows, precision=precise
    )
    return (outputs, state_out)


def strand_core(x_ext, gate_in, b_c, dt_raw, state_in, params):
    dt_bias_h, decay_rate, skip_h, conv_w = params
    conv_out = conv_silu(x_ext, conv_w)
    steps_dt = jax.nn.softplus(dt_raw + dt_bias_h)
    outputs, state_out = block_ssd(
        conv_out, steps_dt, b_c[:, :STATE], b_c[:, STATE:], decay_rate, state_in
    )
    gated = (outputs + skip_h * conv_out) * jax.nn.silu(gate_in)
    return (gated, state_out)


def strand_summary(x_ext, b_c, dt_raw, params):
    dt_bias_h, decay_rate, skip_h, conv_w = params
    conv_out = conv_silu(x_ext, conv_w)
    steps_dt = jax.nn.softplus(dt_raw + dt_bias_h)
    log_keep = jnp.cumsum(steps_dt * decay_rate)
    remains = jnp.exp(log_keep[-1] - log_keep) * steps_dt
    local_state = jnp.einsum("j,jp,jn->pn", remains, conv_out, b_c[:, :STATE], precision=precise)
    return (jnp.exp(log_keep[-1]), local_state)


def chain_step(earlier, following):
    return (earlier[0] * following[0], following[0] * earlier[1] + following[1])


def local(hidden, w_in, w_bc, w_dt, dt_bias, a_log, d_skip, conv_w, w_out, d_out):
    own_rows = hidden.shape[0]
    seq_rows = own_rows * lax.axis_size("tp")
    length_all = seq_rows * lax.axis_size("ctx")
    head_dim = w_out.shape[0]
    rim_rows = CONV - 1
    w_pair = jnp.concatenate([w_in, w_in[::-1]], axis=1)
    bc_pair = jnp.concatenate([w_bc, w_bc[::-1]], axis=1)
    dt_pair = jnp.concatenate([w_dt, w_dt[:, ::-1]], axis=0)
    out_pair = jnp.concatenate([w_out, w_out[:, ::-1]], axis=0)
    params = (dt_bias[0], -jnp.exp(a_log[0]), d_skip[0], conv_w)
    gathered = lax.all_gather(hidden, "tp", axis=0, tiled=True)
    projected = jnp.dot(gathered, w_pair, preferred_element_type=jnp.float32).astype(jnp.bfloat16)
    dt_raw = times_rows(gathered, dt_pair)
    b_c_all = jnp.dot(gathered, bc_pair, preferred_element_type=jnp.float32)
    x_both = jnp.concatenate(
        [projected[:, :head_dim], projected[:, 2 * head_dim : 3 * head_dim]], axis=1
    )
    x_halo = padded(x_both, (("ctx", 0),), rim_rows).astype(jnp.float32)
    x_ext = jnp.stack(
        [x_halo[: seq_rows + rim_rows, :head_dim], x_halo[rim_rows:, head_dim:][::-1]]
    )
    gate_in = jnp.stack(
        [projected[:, head_dim : 2 * head_dim], projected[::-1, 3 * head_dim :]]
    ).astype(jnp.float32)
    b_c = jnp.stack([b_c_all[:, : 2 * STATE], b_c_all[::-1, 2 * STATE :]])
    dt_both = jnp.stack([dt_raw[:, 0], dt_raw[::-1, 1]])
    decays, local_states = jax.vmap(strand_summary, in_axes=(0, 0, 0, None))(
        x_ext, b_c, dt_both, params
    )
    identity = (jnp.ones((), jnp.float32), jnp.zeros((head_dim, STATE), jnp.float32))
    fwd_in = entering((decays[0], local_states[0]), "ctx", chain_step, identity, False)[1]
    rev_in = entering((decays[1], local_states[1]), "ctx", chain_step, identity, True)[1]
    states_in = jnp.stack([fwd_in, rev_in])

    def core_both(x_part, gate_part, bc_part, dt_part, state_part):
        return jax.vmap(strand_core, in_axes=(0, 0, 0, 0, 0, None))(
            x_part, gate_part, bc_part, dt_part, state_part, params
        )

    (gated, states_out), pullback = jax.vjp(core_both, x_ext, gate_in, b_c, dt_both, states_in)
    gated_nat = jnp.concatenate([gated[0], gated[1][::-1]], axis=1).astype(jnp.bfloat16)
    portion = lax.all_gather(d_out, "tp", axis=0, tiled=True)
    grads_g = times_rows(portion, out_pair)
    grad_wout = across_rows(gated_nat, portion)
    grad_stack = jnp.stack([grads_g[:, :head_dim], grads_g[::-1, head_dim:]])
    direct = pullback((grad_stack, jnp.zeros_like(states_out)))
    direct_state = direct[4]
    fwd_adj = entering((decays[0], direct_state[0]), "ctx", chain_step, identity, True)[1]
    rev_adj = entering((decays[1], direct_state[1]), "ctx", chain_step, identity, False)[1]
    carried_grads = pullback((jnp.zeros_like(gated), jnp.stack([fwd_adj, rev_adj])))
    grad_x = direct[0] + carried_grads[0]
    grad_gates = direct[1] + carried_grads[1]
    grad_bcs = direct[2] + carried_grads[2]
    grad_dts = direct[3] + carried_grads[3]
    grad_x_rev = grad_x[1][::-1]
    grad_x_local = jnp.concatenate([grad_x[0][rim_rows:], grad_x_rev[:seq_rows]], axis=1)
    outgoing = jnp.concatenate([grad_x[0][:rim_rows], grad_x_rev[seq_rows:]], axis=0)
    incoming = padded(outgoing, (("ctx", 0),), rim_rows)
    grad_x_local = grad_x_local.at[:rim_rows, head_dim:].add(incoming[:rim_rows])
    grad_x_local = grad_x_local.at[seq_rows - rim_rows :, :head_dim].add(incoming[3 * rim_rows :])
    grad_proj = jnp.concatenate(
        [
            grad_x_local[:, :head_dim],
            grad_gates[0],
            grad_x_local[:, head_dim:],
            grad_gates[1][::-1],
        ],
        axis=1,
    ).astype(jnp.bfloat16)
    grad_bc = jnp.concatenate([grad_bcs[0], grad_bcs[1][::-1]], axis=1).astype(jnp.bfloat16)
    grad_dt = jnp.stack([grad_dts[0], grad_dts[1][::-1]], axis=1).astype(jnp.bfloat16)

    def strand_term(which):
        proj_cols = grad_proj[:, which * 2 * head_dim : (which + 1) * 2 * head_dim]
        wide_cols = w_pair[:, which * 2 * head_dim : (which + 1) * 2 * head_dim]
        bc_cols = grad_bc[:, which * 2 * STATE : (which + 1) * 2 * STATE]
        shared_cols = bc_pair[:, which * 2 * STATE : (which + 1) * 2 * STATE]
        dt_cols = grad_dt[:, which : which + 1]
        dt_rows = dt_pair[which : which + 1]
        summed = times_rows(proj_cols, wide_cols) + times_rows(bc_cols, shared_cols)
        return summed + jnp.dot(dt_cols, dt_rows, preferred_element_type=jnp.float32)

    forward_part = lax.psum_scatter(strand_term(0), "tp", scatter_dimension=0, tiled=True)
    reverse_part = lax.psum_scatter(strand_term(1), "tp", scatter_dimension=0, tiled=True)
    d_hidden = (forward_part + reverse_part).astype(jnp.bfloat16)
    scaling = 1.0 / math.sqrt(length_all)
    grad_pair = across_rows(gathered, grad_proj)
    d_w_in = (grad_pair[:, : 2 * head_dim] + grad_pair[::-1, 2 * head_dim :]) * scaling
    d_w_out = (grad_wout[:head_dim] + grad_wout[head_dim:, ::-1]) * scaling
    d_w_in, d_w_out = (
        lax.psum(d_w_in.astype(jnp.bfloat16), "ctx").astype(jnp.float32),
        lax.psum(d_w_out.astype(jnp.bfloat16), "ctx").astype(jnp.float32),
    )
    grad_bpair = across_rows(gathered, grad_bc)
    d_w_bc = lax.psum(
        (grad_bpair[:, : 2 * STATE] + grad_bpair[::-1, 2 * STATE :]) * scaling, ("ctx", "tp")
    )
    return (d_hidden, d_w_in, d_w_out, d_w_bc)


def solution(mesh):
    in_specs = (
        P(("ctx", "tp"), None),
        P(None, "tp"),
        P(),
        P("tp", None),
        P("tp"),
        P("tp"),
        P("tp"),
        P(None, "tp"),
        P("tp", None),
        P(("ctx", "tp"), None),
    )
    out_specs = (P(("ctx", "tp"), None), P(None, "tp"), P("tp", None), P())
    return jax.shard_map(local, mesh=mesh, in_specs=in_specs, out_specs=out_specs, check_vma=False)
```

profile of v0, /device:TPU:4, one launch (start us, length us, event | category | flops | bytes accessed | tf_op | source)
XLA Modules:
  0.0 1343.6 jit_solution(9077498691237861709)
XLA Ops:
  8.7 6.0 rev.53
  14.8 1.3 convert.70
  18.7 1.3 and_reduce_fusion
  20.6 1.4 slice_bitcast_fusion.12
  22.6 6.3 rev.55
  29.0 8.4 rev.49
  37.4 6.3 rev.51
  43.7 1.3 dynamic-slice.21
  45.7 1.3 dynamic-slice.19
  47.0 85.0 %all-gather.7.cloned.1.call-done = bf16[64,4,2048]{2,1,0:T(4,128)(2,1)} async-done(((bf16[1,4,2048]{2,1,0:T(4,128)(2,1)}), bf16[64,4,2048]{2,1,0:T(4,128)(2,1)}) %all-gather.7.cloned.1.call-update) | async-done | bytes 1048592 | tf_op jit(solution)/shard_map/all_gather | solution.py:119
  132.1 1.3 reshape.271
  138.8 2.1 slice_dynamic-update-slice_fusion
  141.6 107.5 %all-gather.5.cloned.1.call-done = bf16[64,4,2048]{2,1,0:T(4,128)(2,1)} async-done(((bf16[1,4,2048]{2,1,0:T(4,128)(2,1)}), bf16[64,4,2048]{2,1,0:T(4,128)(2,1)}) %all-gather.5.cloned.1.call-update) | async-done | bytes 1048592 | tf_op jit(solution)/shard_map/all_gather | solution.py:150
  249.2 1.3 reshape.269
  250.5 1.5 convolution_bitcast_fusion.2
  253.1 8.6 collective-permute-start
  261.7 1.3 collective-permute-start.1
  263.8 0.9 convolution_add_fusion.9
  264.7 68.7 %all_gather.29 = f32[8,64,16]{1,2,0:T(8,128)S(1)} all-gather(f32[1,64,16]{1,2,0:T(8,128)S(1)} %get-tuple-element.678), channel_id=1, replica_groups=mesh['ctx'=8,'tp'=64] {'ctx'}, dimensions={0}, use_global_device_ids=true | all-gather | bytes 36864 | tf_op jit(solution)/shard_map/all_gather | solution.py:27
  333.4 41.5 %all-reduce.19 = (f32[8]{0:T(128)S(1)}, f32[8]{0:T(128)S(1)}) all-reduce(f32[8]{0:T(128)} %slice_dynamic-update-slice_fusion, f32[8]{0:T(128)} %copy-done.65), channel_id=1, replica_groups=mesh['ctx'=8,'tp'=64] {'ctx'}, use_global_device_ids=true, to_apply=%add.17 | all-reduce | flops 16 | bytes 128
  374.9 10.2 while.62
  385.1 63.2 %all_gather.31 = f32[8,64,16]{1,2,0:T(8,128)S(1)} all-gather(f32[1,64,16]{1,2,0:T(8,128)S(1)} %get-tuple-element.679), channel_id=1, replica_groups=mesh['ctx'=8,'tp'=64] {'ctx'}, dimensions={0}, use_global_device_ids=true | all-gather | bytes 36864 | tf_op jit(solution)/shard_map/all_gather | solution.py:27
  448.3 10.1 while.63
  459.6 0.9 multiply_reduce_fusion.5
  461.9 63.1 %all_gather.32 = f32[8,64,16]{1,2,0:T(8,128)S(1)} all-gather(f32[1,64,16]{1,2,0:T(8,128)S(1)} %get-tuple-element.676), channel_id=1, replica_groups=mesh['ctx'=8,'tp'=64] {'ctx'}, dimensions={0}, use_global_device_ids=true | all-gather | bytes 36864 | tf_op jit(solution)/shard_map/all_gather | solution.py:27
  525.1 10.1 while.64
  535.2 63.3 %all_gather.33 = f32[8,64,16]{1,2,0:T(8,128)S(1)} all-gather(f32[1,64,16]{1,2,0:T(8,128)S(1)} %get-tuple-element.677), channel_id=1, replica_groups=mesh['ctx'=8,'tp'=64] {'ctx'}, dimensions={0}, use_global_device_ids=true | all-gather | bytes 36864 | tf_op jit(solution)/shard_map/all_gather | solution.py:27
  598.4 10.2 while.65
  609.9 1.3 fusion.101
  611.2 1.3 fusion.92
  612.6 1.3 fusion.23
  613.9 1.2 convolution_add_fusion.7
  615.1 1.6 fusion.127
  616.6 1.3 fusion.26
  618.7 1.4 multiply_reduce_fusion.3
  621.3 1.3 copy.40
  622.6 1.3 copy.38
  625.4 1.4 convolution_add_fusion.8
  626.9 1.0 convolution_add_fusion.6
  627.8 2.1 fusion.188
  631.5 2.5 reduce-window.24
  634.9 2.5 reduce-window.26
  639.1 1.1 fusion.112
  640.2 1.3 rev.63
  642.6 0.8 slice.317
  643.4 2.5 collective-permute-start.2
  645.9 1.5 collective-permute-start.3
  648.1 1.1 convolution_bitcast_fusion.1
  649.3 1.9 add_select_fusion
  651.2 2.0 scatter-add.6
  653.2 7.6 collective-permute-done.3
  660.8 1.1 scatter-add.9
  662.0 1.2 convolution_bitcast_fusion
  663.2 1.0 slice.386
  664.2 7.5 rev.61
  671.7 0.9 fusion.10
  672.7 0.8 fusion.157
  673.7 1.2 rev.64
  674.8 1.7 fusion.31
  678.8 453.5 %all-reduce.28 = bf16[256,2048]{1,0:T(8,128)(2,1)S(1)} all-reduce(f32[256,2048]{1,0:T(8,128)S(1)} %fusion.6), channel_id=3, replica_groups=mesh['ctx'=8,'tp'=64] {'tp'}, use_global_device_ids=true, to_apply=%region_27.28.clone | all-reduce | flops 524288 | bytes 3145728
  1133.0 2.2 copy.41
  1135.2 1.8 convert_element_type.39
  1137.0 198.5 %all-reduce.25.cloned.1.call-done = f32[2048,32]{0,1:T(8,128)} async-done(((f32[2048,32]{0,1:T(8,128)}), f32[2048,32]{0,1:T(8,128)}) %all-reduce.25.cloned.1.call-update) | async-done | bytes 262160 | tf_op jit(solution)/shard_map/psum | solution.py:203
  1335.4 1.7 copy.111
  (305 shorter events, 66.8 us)
Async XLA Ops:
  7.2 126.2 %copy-start.27 = (bf16[1,2048]{1,0:T(2,128)(2,1)S(1)}, bf16[1,2048]{1,0:T(2,128)(2,1)}, u32[]{:S(2)}) copy-start(bf16[1,2048]{1,0:T(2,128)(2,1)} %param.25) | copy-start | bytes 12292
  7.2 124.9 %all-gather.7.cloned.1.call-start = ((), (), s32[]{:S(2)}) async-start(), calls=%async_computation.2 | async-start | bytes 1064960 | tf_op jit(solution)/shard_map/all_gather | solution.py:119
  7.9 241.2 %all-gather.5.cloned.1.call-start = ((), (), s32[]{:S(2)}) async-start(), calls=%async_computation.1 | async-start | bytes 1064960 | tf_op jit(solution)/shard_map/all_gather | solution.py:150
  8.7 1124.3 %all-reduce.27.cloned.1.call-start = ((), (), s32[]{:S(2)}) async-start(), calls=%async_computation.3 | async-start | bytes 1572864 | tf_op jit(solution)/shard_map/psum | solution.py:199
  29.0 106.7 %copy-start.5 = (bf16[2048,32]{0,1:T(8,128)(2,1)}, bf16[2048,32]{0,1:T(8,128)(2,1)S(1)}, u32[]{:S(2)}) copy-start(bf16[2048,32]{0,1:T(8,128)(2,1)S(1)} %rev.55) | copy-start | bytes 393220
  37.4 98.3 %copy-start.4 = (bf16[2048,32]{0,1:T(8,128)(2,1)S(1)}, bf16[2048,32]{0,1:T(8,128)(2,1)}, u32[]{:S(2)}) copy-start(bf16[2048,32]{0,1:T(8,128)(2,1)} %param.24) | copy-start | bytes 393220
  43.7 208.6 %copy-start.2 = (bf16[2048,128]{1,0:T(8,128)(2,1)}, bf16[2048,128]{1,0:T(8,128)(2,1)S(1)}, u32[]{:S(2)}) copy-start(bf16[2048,128]{1,0:T(8,128)(2,1)S(1)} %rev.51) | copy-start | bytes 1572868
  134.6 326.7 %copy-start.33 = (f32[256,1]{0,1:T(1,128)}, f32[256,1]{0,1:T(1,128)S(1)}, u32[]{:S(2)}) copy-start(f32[256,1]{0,1:T(1,128)S(1)} %rev.54) | copy-start | bytes 3076
  135.6 116.4 %copy-start.48 = (f32[1,2,2,128]{3,1,2,0:T(2,128)}, f32[1,2,2,128]{3,1,2,0:T(2,128)S(1)}, u32[]{:S(2)}) copy-start(f32[1,2,2,128]{3,1,2,0:T(2,128)S(1)} %copy.67) | copy-start | bytes 6148
  137.7 114.4 %copy-start.63 = (f32[2]{0:T(128)}, f32[2]{0:T(128)S(1)}, u32[]{:S(2)}) copy-start(f32[2]{0:T(128)S(1)} %slice_reduce_fusion.3) | copy-start | bytes 28
  141.6 110.5 %copy-start.65 = (f32[8]{0:T(128)}, f32[8]{0:T(128)S(1)}, u32[]{:S(2)}) copy-start(f32[8]{0:T(128)S(1)} %slice_dynamic-update-slice_fusion.1) | copy-start | bytes 100
  141.6 110.6 %copy-start = (bf16[2048,128]{1,0:T(8,128)(2,1)S(1)}, bf16[2048,128]{1,0:T(8,128)(2,1)}, u32[]{:S(2)}) copy-start(bf16[2048,128]{1,0:T(8,128)(2,1)} %param.23) | copy-start | bytes 1572868
  252.1 11.7 copy-start.15
  252.3 12.4 copy-start.14
  252.3 206.2 %copy-start.34 = (f32[1,256]{1,0:T(1,128)S(1)}, f32[1,256]{1,0:T(1,128)}, u32[]{:S(2)}) copy-start(f32[1,256]{1,0:T(1,128)} %get-tuple-element.686) | copy-start | bytes 3076
  252.8 206.3 %copy-start.42 = (f32[64]{0:T(128)S(1)}, f32[64]{0:T(128)}, u32[]{:S(2)}) copy-start(f32[64]{0:T(128)} %get-tuple-element.689) | copy-start | bytes 772
  252.8 206.3 %copy-start.44 = (f32[64]{0:T(128)S(1)}, f32[64]{0:T(128)}, u32[]{:S(2)}) copy-start(f32[64]{0:T(128)} %get-tuple-element.690) | copy-start | bytes 772
  252.8 206.3 %copy-start.46 = (f32[64]{0:T(128)S(1)}, f32[64]{0:T(128)}, u32[]{:S(2)}) copy-start(f32[64]{0:T(128)} %get-tuple-element.691) | copy-start | bytes 772
  252.8 206.3 %copy-start.53 = (f32[64]{0:T(128)S(1)}, f32[64]{0:T(128)}, u32[]{:S(2)}) copy-start(f32[64]{0:T(128)} %get-tuple-element.688) | copy-start | bytes 772
  252.8 206.8 %copy-start.21 = (f32[256,32]{0,1:T(8,128)S(1)}, f32[256,32]{0,1:T(8,128)}, u32[]{:S(2)}) copy-start(f32[256,32]{0,1:T(8,128)} %rev.56) | copy-start | bytes 98308
  252.8 206.8 %copy-start.23 = (f32[1,256,32]{1,2,0:T(8,128)S(1)}, f32[1,256,32]{1,2,0:T(8,128)}, u32[]{:S(2)}) copy-start(f32[1,256,32]{1,2,0:T(8,128)} %get-tuple-element.672) | copy-start | bytes 98308
  252.9 205.7 %copy-start.24 = (bf16[1,256,64]{1,2,0:T(8,128)(2,1)}, bf16[1,256,64]{1,2,0:T(8,128)(2,1)S(1)}, u32[]{:S(2)}) copy-start(bf16[1,256,64]{1,2,0:T(8,128)(2,1)S(1)} %get-tuple-element.658) | copy-start | bytes 98308
  253.1 205.5 %copy-start.18 = (bf16[256,64]{0,1:T(8,128)(2,1)}, bf16[256,64]{0,1:T(8,128)(2,1)S(1)}, u32[]{:S(2)}) copy-start(bf16[256,64]{0,1:T(8,128)(2,1)S(1)} %rev.52) | copy-start | bytes 98308
  253.1 205.4 %collective-permute-start = (bf16[3,128]{0,1:T(8,128)(2,1)S(1)}, bf16[3,128]{0,1:T(8,128)(2,1)S(1)}, u32[]{:S(2)}, u32[]{:S(2)}) collective-permute-start(bf16[3,128]{0,1:T(8,128)(2,1)S(1)} %get-tuple-element.670), channel_id=1, source_target_pairs={{0,64},{64,128},{128,192},{192,256},{256,320},{320,384},{384,448},... | collective-permute-start | bytes 2312 | tf_op jit(solution)/shard_map/ppermute | solution.py:19
  261.7 196.8 %collective-permute-start.1 = (bf16[3,128]{0,1:T(8,128)(2,1)S(1)}, bf16[3,128]{0,1:T(8,128)(2,1)S(1)}, u32[]{:S(2)}, u32[]{:S(2)}) collective-permute-start(bf16[3,128]{0,1:T(8,128)(2,1)S(1)} %get-tuple-element.671), channel_id=1, source_target_pairs={{64,0},{128,64},{192,128},{256,192},{320,256},{384,320},{448,384},... | collective-permute-start | bytes 2312 | tf_op jit(solution)/shard_map/ppermute | solution.py:20
  263.7 196.8 %copy-start.64 = (f32[2]{0:T(128)S(1)}, f32[2]{0:T(128)}, u32[]{:S(2)}) copy-start(f32[2]{0:T(128)} %copy-done.63) | copy-start | bytes 28
  263.7 197.5 %copy-start.35 = (f32[1,256]{1,0:T(1,128)S(1)}, f32[1,256]{1,0:T(1,128)}, u32[]{:S(2)}) copy-start(f32[1,256]{1,0:T(1,128)} %get-tuple-element.686) | copy-start | bytes 3076
  458.5 140.0 %copy-start.36 = (f32[2,256]{1,0:T(2,128)}, f32[2,256]{1,0:T(2,128)S(1)}, u32[]{:S(2)}) copy-start(f32[2,256]{1,0:T(2,128)S(1)} %compare_select_fusion.3) | copy-start | bytes 6148
  459.3 151.9 %copy-start.19 = (bf16[256,64]{0,1:T(8,128)(2,1)S(1)}, bf16[256,64]{0,1:T(8,128)(2,1)}, u32[]{:S(2)}) copy-start(bf16[256,64]{0,1:T(8,128)(2,1)} %copy-done.18) | copy-start | bytes 98308
  459.4 151.9 %copy-start.25 = (bf16[1,256,64]{1,2,0:T(8,128)(2,1)S(1)}, bf16[1,256,64]{1,2,0:T(8,128)(2,1)}, u32[]{:S(2)}) copy-start(bf16[1,256,64]{1,2,0:T(8,128)(2,1)} %copy-done.24) | copy-start | bytes 98308
  460.5 152.1 %copy-start.28 = (pred[256,256]{1,0:T(8,128)(4,1)S(1)}, pred[256,256]{1,0:T(8,128)(4,1)}, u32[]{:S(2)}) copy-start(pred[256,256]{1,0:T(8,128)(4,1)} %iota_compare_fusion) | copy-start | bytes 196612
  460.5 152.1 %copy-start.49 = (f32[1,2,2,128]{3,1,2,0:T(2,128)S(1)}, f32[1,2,2,128]{3,1,2,0:T(2,128)}, u32[]{:S(2)}) copy-start(f32[1,2,2,128]{3,1,2,0:T(2,128)} %copy-done.48) | copy-start | bytes 6148
  609.6 9.0 copy-start.22
  615.1 3.6 copy-start.29
  615.1 3.6 copy-start.37
  615.1 3.6 copy-start.50
  615.1 3.6 copy-start.54
  625.3 4.7 copy-start.39
  625.3 4.7 copy-start.41
  625.4 4.7 copy-start.55
  625.4 4.7 copy-start.56
  625.4 4.7 copy-start.57
  625.4 4.7 copy-start.58
  625.4 4.7 copy-start.59
  625.4 4.7 copy-start.60
  625.4 4.7 copy-start.61
  625.4 4.7 copy-start.62
  626.8 4.2 copy-start.20
  626.8 4.2 copy-start.26
  626.8 4.2 copy-start.67
  627.8 3.4 copy-start.32
  631.0 31.0 %copy-start.7 = (bf16[256,64]{0,1:T(8,128)(2,1)}, bf16[256,64]{0,1:T(8,128)(2,1)S(1)}, u32[]{:S(2)}) copy-start(bf16[256,64]{0,1:T(8,128)(2,1)S(1)} %rev.58) | copy-start | bytes 98308
  631.3 16.8 %copy-start.16 = (bf16[256,32]{0,1:T(8,128)(2,1)}, bf16[256,32]{0,1:T(8,128)(2,1)S(1)}, u32[]{:S(2)}) copy-start(bf16[256,32]{0,1:T(8,128)(2,1)S(1)} %get-tuple-element.674) | copy-start | bytes 49156
  640.2 7.2 copy-start.51
  640.2 7.2 copy-start.52
  643.4 5.8 collective-permute-start.2
  645.9 14.8 %collective-permute-start.3 = (f32[3,64]{0,1:T(8,128)}, f32[3,64]{0,1:T(8,128)S(1)}, u32[]{:S(2)}, u32[]{:S(2)}) collective-permute-start(f32[3,64]{0,1:T(8,128)} %get-tuple-element.638), channel_id=1, source_target_pairs={{64,0},{128,64},{192,128},{256,192},{320,256},{384,320},{448,384},... | collective-permute-start | bytes 2312 | tf_op jit(solution)/shard_map/ppermute | solution.py:20
  672.7 3.9 copy-start.3
  672.7 3.9 copy-start.8
  672.7 3.9 copy-start.12
  672.7 662.7 %all-reduce.25.cloned.1.call-start = ((), (), s32[]{:S(2)}) async-start(), calls=%async_computation | async-start | bytes 524288 | tf_op jit(solution)/shard_map/psum | solution.py:203
  673.6 3.4 copy-start.1
  673.6 3.5 copy-start.10
  673.6 3.5 copy-start.13
  (13 other events, 21.7 us)
Sparse Core Ops, SparseCore 0:
  10.2 121.8 all-gather.6
  134.2 114.9 all-gather.4
  672.8 200.6 all-reduce.26
  879.7 455.7 all-reduce.24
where the time goes:
time: 1350 us; the launch traced here: 1340 us
  blocking collectives  753 us (56%)
  waiting for transfers between devices  400 us (30%)
  local copies, waits for them, and re-layouts  87.5 us (6%)
  other arithmetic  44.4 us (3%)
  matrix products  25.8 us (2%)
  between operations  17.6 us (1%)
  starting transfers between devices  14 us (1%)
    unnamed x2, blocking collectives  495 us
    all_gather x4, blocking collectives, entering(): everything = jax.tree.map(lambda part: lax.all_gather(part, axis), array)  258 us
    psum x1, waiting for transfers between devices, local(): lax.psum((grad_bpair[:, :2 * STATE] + grad_bpair[::-1, 2 * STATE:]) * sca...  198 us
    all_gather x1, waiting for transfers between devices, local(): portion = lax.all_gather(d_out, 'tp', axis=0, tiled=True)  108 us
    all_gather x1, waiting for transfers between devices, local(): gathered = lax.all_gather(hidden, 'tp', axis=0, tiled=True)  85 us
  transfers between devices with their start and end apart: 8, of which 4 were waited for; matrix products, arithmetic and copies ran while one was open for 6% of the time, Pallas kernels for 0%

commit v1 on v0

--- a/solution.py
+++ b/solution.py
@@ -200,9 +200,10 @@
         lax.psum(d_w_out.astype(jnp.bfloat16), "ctx").astype(jnp.float32),
     )
     grad_bpair = across_rows(gathered, grad_bc)
-    d_w_bc = lax.psum(
-        (grad_bpair[:, : 2 * STATE] + grad_bpair[::-1, 2 * STATE :]) * scaling, ("ctx", "tp")
-    )
+    one_axis = lax.psum(
+        (grad_bpair[:, : 2 * STATE] + grad_bpair[::-1, 2 * STATE :]) * scaling, "tp"
+    )
+    d_w_bc = lax.psum(one_axis, "ctx")
     return (d_hidden, d_w_in, d_w_out, d_w_bc)
 
 

time: 1350 us -> 1950 us (1.44)
  the two profiles are of different devices: /device:TPU:4 before, /device:TPU:256 now
where the time goes in v1:
time: 1950 us; the launch traced here: 1940 us
  waiting for transfers between devices  934 us (48%)
  blocking collectives  792 us (41%)
  local copies, waits for them, and re-layouts  88.4 us (5%)
  other arithmetic  48.6 us (2%)
  matrix products  30.6 us (2%)
  starting transfers between devices  29.5 us (2%)
    psum x1, waiting for transfers between devices, local(): lax.psum((grad_bpair[:, :2 * STATE] + grad_bpair[::-1, 2 * STATE:]) * sca...  737 us
    unnamed x2, blocking collectives  542 us
    all_gather x4, blocking collectives, entering(): everything = jax.tree.map(lambda part: lax.all_gather(part, axis), array)  251 us
    all_gather x1, waiting for transfers between devices, local(): portion = lax.all_gather(d_out, 'tp', axis=0, tiled=True)  108 us
    all_gather x1, waiting for transfers between devices, local(): gathered = lax.all_gather(hidden, 'tp', axis=0, tiled=True)  79.6 us
  transfers between devices with their start and end apart: 9, of which 4 were waited for; matrix products, arithmetic and copies ran while one was open for 5% of the time, Pallas kernels for 0%

profile of v1, /device:TPU:256, one launch (start us, length us, event | category | flops | bytes accessed | tf_op | source)
XLA Modules:
  0.0 1941.8 jit_solution(7818732956382641588)
XLA Ops:
  8.7 6.0 rev.53
  14.8 1.3 convert.70
  18.7 1.3 and_reduce_fusion
  20.7 1.4 slice_bitcast_fusion.12
  22.7 6.3 rev.55
  29.1 8.4 rev.49
  37.5 6.3 rev.51
  43.8 1.3 dynamic-slice.21
  45.8 1.3 dynamic-slice.19
  47.1 79.6 %all-gather.7.cloned.1.call-done = bf16[64,4,2048]{2,1,0:T(4,128)(2,1)} async-done(((bf16[1,4,2048]{2,1,0:T(4,128)(2,1)}), bf16[64,4,2048]{2,1,0:T(4,128)(2,1)}) %all-gather.7.cloned.1.call-update) | async-done | bytes 1048592 | tf_op jit(solution)/shard_map/all_gather | solution.py:119
  126.7 1.3 reshape.271
  132.8 2.0 slice_dynamic-update-slice_fusion
  135.6 108.3 %all-gather.5.cloned.1.call-done = bf16[64,4,2048]{2,1,0:T(4,128)(2,1)} async-done(((bf16[1,4,2048]{2,1,0:T(4,128)(2,1)}), bf16[64,4,2048]{2,1,0:T(4,128)(2,1)}) %all-gather.5.cloned.1.call-update) | async-done | bytes 1048592 | tf_op jit(solution)/shard_map/all_gather | solution.py:150
  243.8 1.3 reshape.269
  245.2 1.5 convolution_bitcast_fusion.2
  247.4 0.9 rev.50
  249.1 7.0 collective-permute-start
  256.2 7.5 collective-permute-start.1
  264.4 0.9 fusion.95
  266.2 63.1 %all_gather.29 = f32[8,64,16]{1,2,0:T(8,128)S(1)} all-gather(f32[1,64,16]{1,2,0:T(8,128)S(1)} %get-tuple-element.678), channel_id=1, replica_groups=mesh['ctx'=8,'tp'=64] {'ctx'}, dimensions={0}, use_global_device_ids=true | all-gather | bytes 36864 | tf_op jit(solution)/shard_map/all_gather | solution.py:27
  329.3 38.8 %all-reduce.19 = (f32[8]{0:T(128)S(1)}, f32[8]{0:T(128)S(1)}) all-reduce(f32[8]{0:T(128)} %slice_dynamic-update-slice_fusion, f32[8]{0:T(128)} %copy-done.51), channel_id=1, replica_groups=mesh['ctx'=8,'tp'=64] {'ctx'}, use_global_device_ids=true, to_apply=%add.17 | all-reduce | flops 16 | bytes 128
  368.1 10.2 while.62
  378.3 61.0 %all_gather.31 = f32[8,64,16]{1,2,0:T(8,128)S(1)} all-gather(f32[1,64,16]{1,2,0:T(8,128)S(1)} %get-tuple-element.679), channel_id=1, replica_groups=mesh['ctx'=8,'tp'=64] {'ctx'}, dimensions={0}, use_global_device_ids=true | all-gather | bytes 36864 | tf_op jit(solution)/shard_map/all_gather | solution.py:27
  439.3 10.1 while.63
  450.1 0.9 fusion.74
  451.2 1.6 multiply_reduce_fusion.5
  454.3 63.1 %all_gather.32 = f32[8,64,16]{1,2,0:T(8,128)S(1)} all-gather(f32[1,64,16]{1,2,0:T(8,128)S(1)} %get-tuple-element.676), channel_id=1, replica_groups=mesh['ctx'=8,'tp'=64] {'ctx'}, dimensions={0}, use_global_device_ids=true | all-gather | bytes 36864 | tf_op jit(solution)/shard_map/all_gather | solution.py:27
  517.3 10.1 while.64
  527.5 63.2 %all_gather.33 = f32[8,64,16]{1,2,0:T(8,128)S(1)} all-gather(f32[1,64,16]{1,2,0:T(8,128)S(1)} %get-tuple-element.677), channel_id=1, replica_groups=mesh['ctx'=8,'tp'=64] {'ctx'}, dimensions={0}, use_global_device_ids=true | all-gather | bytes 36864 | tf_op jit(solution)/shard_map/all_gather | solution.py:27
  590.7 10.2 while.65
  601.0 1.0 fusion.153
  602.0 0.9 fusion.142
  602.9 1.3 fusion.101
  604.2 1.3 fusion.92
  605.5 2.2 fusion.23
  607.7 2.0 convolution_add_fusion.7
  609.8 2.2 fusion.127
  612.0 1.3 fusion.26
  615.0 1.7 convolution_add_fusion.3
  616.7 3.2 multiply_reduce_fusion.3
  621.3 2.5 reduce-window.24
  625.5 2.5 reduce-window.26
  632.2 1.2 broadcast_multiply_fusion
  634.1 1.1 add_add_fusion
  635.2 1.3 convolution_add_fusion.8
  640.2 1.2 rev.64
  642.2 1.1 fusion.112
  643.4 1.3 rev.63
  645.4 1.0 slice_bitcast_fusion.4
  647.5 10.4 collective-permute-start.2
  657.9 4.3 collective-permute-start.3
  662.3 2.1 add_select_fusion
  664.4 2.1 scatter-add.6
  666.5 7.3 collective-permute-done.3
  673.9 1.1 scatter-add.9
  675.5 1.0 slice.386
  676.5 7.5 rev.61
  684.0 0.9 fusion.10
  684.9 1.6 fusion.108
  688.4 737.5 %all-reduce.26.cloned.1.call-done = f32[2048,32]{0,1:T(8,128)} async-done(((f32[2048,32]{0,1:T(8,128)}), f32[2048,32]{0,1:T(8,128)}) %all-reduce.26.cloned.1.call-update) | async-done | bytes 262160 | tf_op jit(solution)/shard_map/psum | solution.py:203
  1425.9 503.0 %all-reduce.31 = bf16[256,2048]{1,0:T(8,128)(2,1)S(1)} all-reduce(f32[256,2048]{1,0:T(8,128)S(1)} %fusion.6), channel_id=3, replica_groups=mesh['ctx'=8,'tp'=64] {'tp'}, use_global_device_ids=true, to_apply=%region_27.28.clone | all-reduce | flops 524288 | bytes 3145728
  1929.6 2.2 copy.41
  1931.8 1.8 convert_element_type.39
  1933.6 1.7 copy.112
  (283 shorter events, 72.7 us)
Async XLA Ops:
  7.2 120.9 %copy-start.18 = (bf16[1,2048]{1,0:T(2,128)(2,1)S(1)}, bf16[1,2048]{1,0:T(2,128)(2,1)}, u32[]{:S(2)}) copy-start(bf16[1,2048]{1,0:T(2,128)(2,1)} %param.25) | copy-start | bytes 12292
  7.2 119.5 %all-gather.7.cloned.1.call-start = ((), (), s32[]{:S(2)}) async-start(), calls=%async_computation.3 | async-start | bytes 1064960 | tf_op jit(solution)/shard_map/all_gather | solution.py:119
  7.9 235.9 %all-gather.5.cloned.1.call-start = ((), (), s32[]{:S(2)}) async-start(), calls=%async_computation.2 | async-start | bytes 1064960 | tf_op jit(solution)/shard_map/all_gather | solution.py:150
  8.7 1417.3 %all-reduce.26.cloned.1.call-start = ((), (), s32[]{:S(2)}) async-start(), calls=%async_computation | async-start | bytes 524288 | tf_op jit(solution)/shard_map/psum | solution.py:203
  37.5 92.2 %copy-start.3 = (bf16[2048,32]{0,1:T(8,128)(2,1)S(1)}, bf16[2048,32]{0,1:T(8,128)(2,1)}, u32[]{:S(2)}) copy-start(bf16[2048,32]{0,1:T(8,128)(2,1)} %param.24) | copy-start | bytes 393220
  43.8 205.0 %copy-start.2 = (bf16[2048,128]{1,0:T(8,128)(2,1)}, bf16[2048,128]{1,0:T(8,128)(2,1)S(1)}, u32[]{:S(2)}) copy-start(bf16[2048,128]{1,0:T(8,128)(2,1)S(1)} %rev.51) | copy-start | bytes 1572868
  128.4 321.0 %copy-start.25 = (f32[1,256]{1,0:T(1,128)}, f32[1,256]{1,0:T(1,128)S(1)}, u32[]{:S(2)}) copy-start(f32[1,256]{1,0:T(1,128)S(1)} %get-tuple-element.686) | copy-start | bytes 3076
  129.7 117.0 %copy-start.34 = (f32[1,2,2,128]{3,1,2,0:T(2,128)}, f32[1,2,2,128]{3,1,2,0:T(2,128)S(1)}, u32[]{:S(2)}) copy-start(f32[1,2,2,128]{3,1,2,0:T(2,128)S(1)} %copy.67) | copy-start | bytes 6148
  131.7 115.7 %copy-start.47 = (f32[2]{0:T(128)}, f32[2]{0:T(128)S(1)}, u32[]{:S(2)}) copy-start(f32[2]{0:T(128)S(1)} %slice_reduce_fusion.3) | copy-start | bytes 28
  135.5 111.8 %copy-start.51 = (f32[8]{0:T(128)}, f32[8]{0:T(128)S(1)}, u32[]{:S(2)}) copy-start(f32[8]{0:T(128)S(1)} %slice_dynamic-update-slice_fusion.1) | copy-start | bytes 100
  135.6 112.7 %copy-start = (bf16[2048,128]{1,0:T(8,128)(2,1)S(1)}, bf16[2048,128]{1,0:T(8,128)(2,1)}, u32[]{:S(2)}) copy-start(bf16[2048,128]{1,0:T(8,128)(2,1)} %param.23) | copy-start | bytes 1572868
  248.8 200.7 %copy-start.12 = (bf16[1,256,64]{1,2,0:T(8,128)(2,1)}, bf16[1,256,64]{1,2,0:T(8,128)(2,1)S(1)}, u32[]{:S(2)}) copy-start(bf16[1,256,64]{1,2,0:T(8,128)(2,1)S(1)} %get-tuple-element.658) | copy-start | bytes 98308
  249.0 17.1 copy-start.7
  249.1 200.4 %collective-permute-start = (bf16[3,128]{0,1:T(8,128)(2,1)S(1)}, bf16[3,128]{0,1:T(8,128)(2,1)S(1)}, u32[]{:S(2)}, u32[]{:S(2)}) collective-permute-start(bf16[3,128]{0,1:T(8,128)(2,1)S(1)} %get-tuple-element.670), channel_id=1, source_target_pairs={{0,64},{64,128},{128,192},{192,256},{256,320},{320,384},{384,448},... | collective-permute-start | bytes 2312 | tf_op jit(solution)/shard_map/ppermute | solution.py:19
  256.2 193.4 %collective-permute-start.1 = (bf16[3,128]{0,1:T(8,128)(2,1)S(1)}, bf16[3,128]{0,1:T(8,128)(2,1)S(1)}, u32[]{:S(2)}, u32[]{:S(2)}) collective-permute-start(bf16[3,128]{0,1:T(8,128)(2,1)S(1)} %get-tuple-element.671), channel_id=1, source_target_pairs={{64,0},{128,64},{192,128},{256,192},{320,256},{384,320},{448,384},... | collective-permute-start | bytes 2312 | tf_op jit(solution)/shard_map/ppermute | solution.py:20
  264.4 188.4 %copy-start.48 = (f32[2]{0:T(128)S(1)}, f32[2]{0:T(128)}, u32[]{:S(2)}) copy-start(f32[2]{0:T(128)} %copy-done.47) | copy-start | bytes 28
  449.5 141.2 %copy-start.28 = (f32[2,256]{1,0:T(2,128)}, f32[2,256]{1,0:T(2,128)S(1)}, u32[]{:S(2)}) copy-start(f32[2,256]{1,0:T(2,128)S(1)} %compare_select_fusion.3) | copy-start | bytes 6148
  449.5 4.1 copy-start.26
  451.0 153.2 %copy-start.8 = (bf16[256,64]{0,1:T(8,128)(2,1)S(1)}, bf16[256,64]{0,1:T(8,128)(2,1)}, u32[]{:S(2)}) copy-start(bf16[256,64]{0,1:T(8,128)(2,1)} %copy-done.7) | copy-start | bytes 98308
  451.0 153.2 %copy-start.13 = (bf16[1,256,64]{1,2,0:T(8,128)(2,1)S(1)}, bf16[1,256,64]{1,2,0:T(8,128)(2,1)}, u32[]{:S(2)}) copy-start(bf16[1,256,64]{1,2,0:T(8,128)(2,1)} %copy-done.12) | copy-start | bytes 98308
  451.2 2.4 copy-start.54
  452.8 0.8 copy-start.30
  452.8 0.8 copy-start.32
  452.8 149.2 %copy-start.16 = (f32[2,256,16]{1,2,0:T(8,128)}, f32[2,256,16]{1,2,0:T(8,128)S(1)}, u32[]{:S(2)}) copy-start(f32[2,256,16]{1,2,0:T(8,128)S(1)} %get-tuple-element.633) | copy-start | bytes 98308
  600.9 8.9 copy-start.19
  600.9 8.9 copy-start.35
  602.9 6.9 copy-start.17
  607.7 5.6 copy-start.50
  607.7 6.3 copy-start.49
  609.8 6.9 copy-start.29
  614.9 5.0 copy-start.31
  614.9 5.0 copy-start.33
  614.9 5.0 copy-start.39
  614.9 5.0 copy-start.40
  614.9 5.0 copy-start.41
  614.9 5.0 copy-start.42
  614.9 5.0 copy-start.44
  614.9 5.0 copy-start.45
  615.0 15.3 copy-start.27
  628.8 6.4 copy-start.20
  628.8 6.4 copy-start.53
  632.2 4.4 copy-start.24
  632.2 4.6 copy-start.4
  632.2 4.6 copy-start.9
  632.2 4.6 copy-start.11
  632.2 4.6 copy-start.14
  632.2 4.6 copy-start.36
  632.2 4.6 copy-start.52
  636.5 2.0 copy-start.10
  636.5 2.0 copy-start.15
  636.5 2.0 copy-start.38
  636.5 2.0 copy-start.55
  636.8 2.0 copy-start.23
  636.8 2.2 copy-start.46
  638.8 4.5 copy-start.5
  642.2 1287.4 %all-reduce.30.cloned.1.call-start = ((), (), s32[]{:S(2)}) async-start(), calls=%async_computation.4 | async-start | bytes 1572864 | tf_op jit(solution)/shard_map/psum | solution.py:199
  647.5 14.8 collective-permute-start.2
  657.9 15.9 collective-permute-start.3
  684.9 1.7 copy-start.1
  686.5 0.7 copy-start.22
  686.5 1247.0 %all-reduce.28.cloned.1.call-start = ((), (), s32[]{:S(2)}) async-start(), calls=%async_computation.1 | async-start | bytes 524288 | tf_op jit(solution)/shard_map/psum | solution.py:206
  687.2 0.7 copy-start.6
  687.2 0.7 copy-start.21
  687.2 0.7 copy-start.37
  (1 other events, 0.7 us)
Sparse Core Ops, SparseCore 0:
  10.2 116.4 all-gather.6
  128.8 114.9 all-gather.4
  642.3 783.5 all-reduce.25
  1429.6 199.0 all-reduce.29
  1631.5 145.4 all-reduce.27
